TPU v7x, 32 devices: a whole 2x2x4 slice. The times are simulated.
32 devices in a mesh: group: 2 (over y), batch: 4 (over z), mp: 2 (over x), section: 2 (over core).
Axes of the slice: x: 2, y: 2, z: 4, core: 2. Of those that a mesh axis runs over, the one named last changes fastest.
Arguments:
- queries: bfloat16 [2, 192, 8192], P('section', ('group', 'batch'), 'mp'), parts along dimension 1, may hold values from -6 to 6
- new_keys: bfloat16 [2, 192, 1024], P('section', ('group', 'batch'), 'mp'), parts along dimension 1, may hold values from -6 to 6
- new_values: bfloat16 [2, 192, 1024], P('section', ('group', 'batch'), 'mp'), parts along dimension 1, may hold values from -6 to 6
- key_pages: bfloat16 [2, 768, 16, 1024], P('section', ('group', 'batch'), None, 'mp'), parts along dimension 1, may hold values from -6 to 6
- value_pages: bfloat16 [2, 768, 16, 1024], P('section', ('group', 'batch'), None, 'mp'), parts along dimension 1, may hold values from -6 to 6
- page_table: int32 [192, 4], P(('group', 'batch')), parts along dimension 0, may hold values from 0 to 95, as said below
- ancestry: int32 [192], P('group'), parts along dimension 0, may hold values from 0 to 95, as said below
- lengths: int32 [192], P('group'), parts along dimension 0, may hold values from 1 to 64, as said below
- step_rows: bfloat16 [8192, 4096], P(('group', 'batch', 'section'), 'mp'), parts along dimension 0, may hold values from -6 to 6
- norm_gain: float32 [4096], replicated, may hold values from 0.1 to 1.9
- head_weight: bfloat16 [4096, 4096], P(('batch', 'section'), 'mp'), may hold values from -0.09375 to 0.09375
- head_bias: float32 [4096], P('mp'), may hold values from -5 to 5
- class_weight: bfloat16 [4096, 2], P('mp'), may hold values from -0.125 to 0.125
- class_bias: float32 [2], replicated, may hold values from -4 to 4
Outputs:
- attention: bfloat16 [2, 192, 8192], P('section', ('group', 'batch'), 'mp'), parts along dimension 1
- log_odds: float32 [8192], P(('group', 'batch', 'section')), parts along dimension 0
There are 2 independent parts, one for each index of `group`. A program takes and returns all parts, laid end to end along the dimension named above; an argument that names none is the same for every part. Nothing has to cross between parts.
Inputs may be any that keep to these rules, and one draw needn't show every extreme that they name: The pages of the particles on one index of batch lie on that index; the page_table rows of those 24 particles name each of its 96 pages exactly once. Particle j belongs to problem j % 24, and ancestry[j] % 24 == j % 24. Particles j // 24 == d stand on index d of batch; the 24 slots on one index take at most 12 ancestors from any one index, and in every draw some index gives exactly 12 ancestors to the slots of every index. `lengths`: some particle has all 64 positions live in every draw.
All inputs are finite; a program needn't handle non-finite values.
Results may differ from a plain program's by a relative error of at most 0.0043.
Values may be sent and summed in bfloat16 or wider, within the bound.
A program may use at most 64 MiB of HBM per device.

v0:
```python
import jax
import jax.numpy as jnp
from jax import lax
from jax.sharding import PartitionSpec as P

HD = 128


def cache_score_terms(query_head_count, cached_key_rows, cache_values, live_lengths):
    score_scale = 1.0 / HD**0.5
    attention_scores = (
        jnp.einsum(
            "bkgd,btkd->bkgt", query_head_count, cached_key_rows, preferred_element_type=jnp.float32
        )
        * score_scale
    )
    live_mask = jnp.arange(cached_key_rows.shape[1])[None, :] < live_lengths[:, None]
    attention_scores = jnp.where(live_mask[:, None, None, :], attention_scores, -1e30)
    top_score = jnp.max(attention_scores, axis=-1)
    weights = jnp.exp(attention_scores - top_score[..., None])
    denominator = jnp.sum(weights, axis=-1)
    numerator = jnp.einsum(
        "bkgt,btkd->bkgd",
        weights.astype(jnp.bfloat16),
        cache_values,
        preferred_element_type=jnp.float32,
    )
    return (numerator, top_score, denominator)


def finish(numerator, top_score, denominator, query_head_count, particle_key_rows, own_values):
    score_scale = 1.0 / HD**0.5
    own_score = (
        jnp.einsum(
            "vnrc,vnc->vnr", query_head_count, particle_key_rows, preferred_element_type=jnp.float32
        )
        * score_scale
    )
    own_weight = jnp.exp(own_score - top_score)
    result = (numerator + own_weight[..., None] * own_values.astype(jnp.float32)[:, :, None, :]) / (
        denominator + own_weight
    )[..., None]
    return result.astype(jnp.bfloat16)


def per_device(
    queries,
    new_keys,
    new_values,
    key_pages,
    value_pages,
    page_table,
    ancestry,
    lengths,
    step_rows,
    norm_gain,
    head_weight,
    head_bias,
    class_weight,
    class_bias,
):
    layer_count = queries.shape[0]
    slot_count = page_table.shape[0]
    page_count = page_table.shape[1]
    page_size = key_pages.shape[2]
    kv_width = key_pages.shape[3]
    kv_local = kv_width // HD
    group_size = queries.shape[2] // kv_width
    context = page_count * page_size
    device_count = lax.axis_size("batch")
    my_index = lax.axis_index("batch")
    capacity = max(2, (2 * slot_count + device_count - 1) // device_count)
    source = (ancestry // slot_count).reshape(device_count, slot_count)
    positions = jnp.arange(slot_count)
    earlier = positions[None, :] < positions[:, None]
    same_source = source[:, :, None] == source[:, None, :]
    source_rank = jnp.sum(same_source & earlier[None, :, :], axis=2)
    slot_ids = jnp.arange(capacity)
    served = (source == my_index)[:, None, :] & (source_rank[:, None, :] == slot_ids[None, :, None])
    served_slot = jnp.sum(jnp.where(served, positions[None, None, :], 0), axis=2)
    own_source = lax.dynamic_index_in_dim(source, my_index, 0, keepdims=False)
    own_rank = lax.dynamic_index_in_dim(source_rank, my_index, 0, keepdims=False)
    flat_index = own_source * capacity + own_rank
    local_lengths = lax.dynamic_slice_in_dim(lengths, my_index * slot_count, slot_count)
    query_head_count = queries.reshape(layer_count * slot_count, kv_local, group_size, HD)
    particle_key_rows = new_keys.reshape(layer_count * slot_count, kv_local, HD)
    own_values = new_values.reshape(layer_count * slot_count, kv_local, HD)
    served_pages = page_table[served_slot]
    wanted = (own_source[None, None, :] == jnp.arange(device_count)[:, None, None]) & (
        own_rank[None, None, :] == slot_ids[None, :, None]
    )
    request_slot = jnp.sum(jnp.where(wanted, positions[None, None, :], 0), axis=2)
    outgoing_queries = jnp.take(queries, request_slot, axis=1)
    arrived_queries = lax.all_to_all(
        outgoing_queries, "batch", split_axis=1, concat_axis=1, tiled=True
    )
    batch_rows = layer_count * device_count * capacity
    served_heads = arrived_queries.reshape(batch_rows, kv_local, group_size, HD)
    served_keys = key_pages[:, served_pages].reshape(batch_rows, context, kv_local, HD)
    served_values = value_pages[:, served_pages].reshape(batch_rows, context, kv_local, HD)
    served_lengths = jnp.tile(
        jnp.take(local_lengths, served_slot).reshape(device_count * capacity), layer_count
    )
    numerator, top_score, denominator = cache_score_terms(
        served_heads, served_keys, served_values, served_lengths
    )
    numerator = numerator.reshape(layer_count, device_count, capacity, kv_local * group_size * HD)
    top_score = top_score.reshape(layer_count, device_count, capacity, kv_local * group_size)
    denominator = denominator.reshape(layer_count, device_count, capacity, kv_local * group_size)
    returned = (
        lax.all_to_all(numerator, "batch", split_axis=1, concat_axis=1, tiled=True),
        lax.all_to_all(top_score, "batch", split_axis=1, concat_axis=1, tiled=True),
        lax.all_to_all(denominator, "batch", split_axis=1, concat_axis=1, tiled=True),
    )

    def pick_part(received, trailing):
        received = received.reshape((layer_count, device_count * capacity) + trailing)
        return jnp.take(received, flat_index, axis=1).reshape(
            (layer_count * slot_count,) + trailing
        )

    numerator = pick_part(returned[0], (kv_local, group_size, HD))
    top_score = pick_part(returned[1], (kv_local, group_size))
    denominator = pick_part(returned[2], (kv_local, group_size))
    result = finish(
        numerator, top_score, denominator, query_head_count, particle_key_rows, own_values
    )
    attention = result.reshape(layer_count, slot_count, kv_local * group_size * HD)
    full_rows = lax.all_gather(step_rows, "mp", axis=1, tiled=True)
    row_values = full_rows.astype(jnp.float32)
    power = jnp.mean(row_values * row_values, axis=1, keepdims=True)
    normed = (row_values * lax.rsqrt(power + 1e-06) * norm_gain).astype(jnp.bfloat16)
    projected = jnp.dot(
        normed,
        lax.all_gather(head_weight, ("batch", "section"), axis=0, tiled=True),
        preferred_element_type=jnp.float32,
    )
    hidden = jnp.maximum(projected + head_bias, 0.0).astype(jnp.bfloat16)
    partial_logits = jnp.dot(hidden, class_weight, preferred_element_type=jnp.float32)
    logits = lax.psum(partial_logits, "mp") + class_bias
    log_odds = logits[:, 1] - logits[:, 0]
    return (attention, log_odds)


def solution(mesh):
    placed = (
        P("section", ("group", "batch"), "mp"),
        P("section", ("group", "batch"), "mp"),
        P("section", ("group", "batch"), "mp"),
        P("section", ("group", "batch"), None, "mp"),
        P("section", ("group", "batch"), None, "mp"),
        P(("group", "batch"), None),
        P("group"),
        P("group"),
        P(("group", "batch", "section"), "mp"),
        P(),
        P(("batch", "section"), "mp"),
        P("mp"),
        P("mp", None),
        P(),
    )
    return jax.shard_map(
        per_device,
        mesh=mesh,
        in_specs=placed,
        out_specs=(P("section", ("group", "batch"), "mp"), P(("group", "batch", "section"))),
        check_vma=False,
    )
```

profile of v0, /device:TPU:0, one launch (start us, length us, event | category | flops | bytes accessed | tf_op | source)
XLA Modules:
  0.0 253.1 jit_solution(18221568556298894525)
XLA Ops:
  10.2 0.8 gather_fusion.1
  11.1 0.9 select_bitcast_fusion
  12.0 6.3 %all-to-all-start = ((bf16[1,4,12,4096]{3,2,0,1:T(8,128)(2,1)}), bf16[1,4,12,4096]{3,2,0,1:T(8,128)(2,1)}, u32[]{:S(2)}, u32[]{:S(2)}) async-start(bf16[1,4,12,4096]{3,2,0,1:T(8,128)(2,1)} %select_bitcast_fusion), calls=%async_computation | async-start | bytes 1048576 | tf_op jit(solution)/shard_map/all_to_all | solution.py:94
  19.9 0.8 gather_fusion
  20.9 2.7 %gather_fusion.3 = bf16[192,16,512]{2,1,0:T(8,128)(2,1)} fusion(bf16[96,16,512]{2,1,0:T(8,128)(2,1)S(1)} %bitcast.71, s32[1024]{0:T(1024)S(1)} %pad_clamp_fusion.2), kind=kCustom, calls=%fused_computation.5 | custom fusion | bytes 6292224 | tf_op jit(solution)/shard_map/gather | solution.py:99
  23.6 5.6 %reshape.355 = bf16[48,64,4,128]{3,2,1,0:T(4,128)(2,1)} reshape(bf16[192,16,512]{2,1,0:T(8,128)(2,1)} %gather_fusion.3) | data formatting | bytes 6291456 | tf_op jit(solution)/shard_map/reshape | solution.py:99
  29.3 3.6 %all-to-all-done = bf16[1,4,12,4096]{3,2,0,1:T(8,128)(2,1)} async-done(((bf16[1,4,12,4096]{3,2,0,1:T(8,128)(2,1)}), bf16[1,4,12,4096]{3,2,0,1:T(8,128)(2,1)}, u32[]{:S(2)}, u32[]{:S(2)}) %all-to-all-start) | async-done | bytes 393248 | tf_op jit(solution)/shard_map/all_to_all | solution.py:94
  33.0 2.1 reshape.354
  35.0 3.9 %fusion.35 = (f32[48,4,8]{2,1,0:T(4,128)S(1)}, f32[48,4,8,64]{3,2,1,0:T(8,128)S(1)}) fusion(bf16[48,4,8,128]{3,2,1,0:T(8,128)(2,1)} %reshape.354, bf16[48,64,4,128]{3,2,1,0:T(4,128)(2,1)} %reshape.355, pred[48,64]{1,0:T(8,128)(4,1)S(1)} %iota_compare_fusion.1), kind=kOutput, calls=%fused_computation.71 | convolution fusion | flops 25459200 | bytes 3941376 | tf_op jit(solution)/shard_map/bkgd,btkd->bkgt/dot_general | solution.py:12
  38.9 0.9 copy-done.3
  40.4 0.7 reshape.479
  41.7 1.5 reduce.4
  43.9 3.2 %all-to-all-start.3 = ((f32[4,1,384]{2,1,0:T(1,128)}), f32[4,1,384]{2,1,0:T(1,128)S(1)}, u32[]{:S(2)}, u32[]{:S(2)}) async-start(f32[4,1,384]{2,1,0:T(1,128)} %reshape.484), calls=%async_computation.3 | async-start | bytes 12288 | tf_op jit(solution)/shard_map/all_to_all | solution.py:113
  47.1 2.7 %gather_fusion.4 = bf16[192,16,512]{2,1,0:T(8,128)(2,1)} fusion(bf16[96,16,512]{2,1,0:T(8,128)(2,1)S(1)} %bitcast.74, s32[1024]{0:T(1024)S(1)} %pad_clamp_fusion.2), kind=kCustom, calls=%fused_computation.6 | custom fusion | bytes 6292224 | tf_op jit(solution)/shard_map/gather | solution.py:100
  49.8 5.6 %reshape.356 = bf16[48,64,4,128]{3,2,1,0:T(4,128)(2,1)} reshape(bf16[192,16,512]{2,1,0:T(8,128)(2,1)} %gather_fusion.4) | data formatting | bytes 6291456 | tf_op jit(solution)/shard_map/reshape | solution.py:100
  55.6 0.7 reduce.6
  57.0 5.0 %all-to-all-start.2 = ((f32[4,1,384]{2,1,0:T(1,128)}), f32[4,1,384]{2,1,0:T(1,128)S(1)}, u32[]{:S(2)}, u32[]{:S(2)}) async-start(f32[4,1,384]{2,1,0:T(1,128)} %reshape.482), calls=%async_computation.2 | async-start | bytes 12288 | tf_op jit(solution)/shard_map/all_to_all | solution.py:112
  62.1 3.8 %fusion.9 = f32[48,4,8,128]{3,2,1,0:T(8,128)} fusion(bf16[48,64,4,128]{3,2,1,0:T(4,128)(2,1)} %reshape.356, f32[48,4,8,64]{3,2,1,0:T(8,128)S(1)} %copy-done.4, f32[48,4,8]{2,1,0:T(4,128)S(1)} %get-tuple-element.9), kind=kOutput, calls=%fused_computation.17 | convolution fusion | flops 25362432 | bytes 4331520 | tf_op jit(solution)/shard_map/bkgt,btkd->bkgd/dot_general | solution.py:22
  65.9 1.8 all-to-all-done.2
  67.6 3.7 %all-to-all-start.1 = ((f32[1,4,12,4096]{3,0,2,1:T(1,128)}), f32[1,4,12,4096]{3,0,2,1:T(1,128)S(1)}, u32[]{:S(2)}, u32[]{:S(2)}) async-start(f32[1,4,12,4096]{3,0,2,1:T(1,128)} %bitcast.8), calls=%async_computation.1 | async-start | bytes 1572864 | tf_op jit(solution)/shard_map/all_to_all | solution.py:111
  71.7 0.7 reduce.7
  72.6 0.7 reduce.5
  75.3 0.9 broadcast_multiply_fusion
  76.2 1.1 mul.82
  77.3 27.7 %all-to-all-done.1 = f32[1,4,12,4096]{3,0,2,1:T(1,128)S(1)} async-done(((f32[1,4,12,4096]{3,0,2,1:T(1,128)}), f32[1,4,12,4096]{3,0,2,1:T(1,128)S(1)}, u32[]{:S(2)}, u32[]{:S(2)}) %all-to-all-start.1) | async-done | bytes 786464 | tf_op jit(solution)/shard_map/all_to_all | solution.py:111
  105.0 1.3 gather_fusion.5
  106.4 1.1 gather.38
  107.5 0.8 divide_convert_fusion
  108.3 3.2 %fusion = f32[512]{0:T(512)S(1)} fusion(bf16[512,4096]{1,0:T(8,128)(2,1)} %all-gather.3.cloned.1.call-done), kind=kLoop, calls=%fused_computation.10 | loop fusion | flops 6290944 | bytes 4196352 | tf_op jit(solution)/shard_map/reduce_sum | solution.py:131
  111.5 115.2 %all-gather.5.cloned.1.call-done = bf16[4096,2048]{1,0:T(8,128)(2,1)} async-done(((bf16[512,2048]{1,0:T(8,128)(2,1)}), bf16[4096,2048]{1,0:T(8,128)(2,1)}) %all-gather.5.cloned.1.call-update) | async-done | bytes 16777232 | tf_op jit(solution)/shard_map/all_gather | solution.py:135
  226.6 14.0 %fusion.20 = f32[512,2]{0,1:T(2,128)S(1)} fusion(bf16[2048,2]{0,1:T(2,128)(2,1)S(1)} %copy-done.11, bf16[4096,2048]{1,0:T(8,128)(2,1)} %all-gather.5.cloned.1.call-done, bf16[512,4096]{1,0:T(8,128)(2,1)} %all-gather.3.cloned.1.call-done, f32[4096]{0:T(1024)S(1)} %copy-done.10, f32[512]{0:T(512)S(1)} %add_rsqrt_fusion, f32[2048]{0:T(1024)S(1)} %copy-done.12), kind=kOutput, calls=%fused_computation.23 | convolution fusion | flops 8605663232 | bytes 21010432 | tf_op jit(solution)/shard_map/dot_general | solution.py:139
  240.7 4.9 %psum.7 = f32[512,2]{0,1:T(2,128)S(1)} all-reduce(f32[512,2]{0,1:T(2,128)S(1)} %fusion.20), channel_id=1, replica_groups=mesh['group'=2,'batch'=4,'mp'=2,'section'=2] {'mp'}, use_global_device_ids=true, to_apply=%region_6.8 | all-reduce | flops 1024 | bytes 8192 | tf_op jit(solution)/shard_map/psum | solution.py:140
  (94 shorter events, 10.6 us)
Async XLA Ops:
  7.2 13.7 %copy-start = (bf16[1,96,16,512]{3,2,1,0:T(8,128)(2,1)S(1)}, bf16[1,96,16,512]{3,2,1,0:T(8,128)(2,1)}, u32[]{:S(2)}) copy-start(bf16[1,96,16,512]{3,2,1,0:T(8,128)(2,1)} %param.19) | copy-start | bytes 4718596
  7.2 1.5 copy-start.13
  7.2 3.0 %copy-start.1 = (bf16[1,24,4096]{2,1,0:T(8,128)(2,1)S(1)}, bf16[1,24,4096]{2,1,0:T(8,128)(2,1)}, u32[]{:S(2)}) copy-start(bf16[1,24,4096]{2,1,0:T(8,128)(2,1)} %param.16) | copy-start | bytes 589828
  7.2 101.1 %all-gather.3.cloned.1.call-start = ((), (), s32[]{:S(2)}) async-start(), calls=%async_computation.4 | async-start | bytes 6291456 | tf_op jit(solution)/shard_map/all_gather | solution.py:129
  7.9 218.7 %all-gather.5.cloned.1.call-start = ((), (), s32[]{:S(2)}) async-start(), calls=%async_computation.5 | async-start | bytes 18874368 | tf_op jit(solution)/shard_map/all_gather | solution.py:135
  10.2 8.7 %copy-start.7 = (s32[24,4]{0,1:T(4,128)S(1)}, s32[24,4]{0,1:T(4,128)}, u32[]{:S(2)}) copy-start(s32[24,4]{0,1:T(4,128)} %param.21) | copy-start | bytes 1156
  10.2 9.6 %copy-start.14 = (s32[96]{0:T(128)S(1)}, s32[96]{0:T(128)}, u32[]{:S(2)}) copy-start(s32[96]{0:T(128)} %param.23) | copy-start | bytes 1156
  12.0 20.9 %all-to-all-start = ((bf16[1,4,12,4096]{3,2,0,1:T(8,128)(2,1)}), bf16[1,4,12,4096]{3,2,0,1:T(8,128)(2,1)}, u32[]{:S(2)}, u32[]{:S(2)}) async-start(bf16[1,4,12,4096]{3,2,0,1:T(8,128)(2,1)} %select_bitcast_fusion), calls=%async_computation | async-start | bytes 1048576 | tf_op jit(solution)/shard_map/all_to_all | solution.py:94
  29.3 17.8 %copy-start.2 = (bf16[1,96,16,512]{3,2,1,0:T(8,128)(2,1)S(1)}, bf16[1,96,16,512]{3,2,1,0:T(8,128)(2,1)}, u32[]{:S(2)}) copy-start(bf16[1,96,16,512]{3,2,1,0:T(8,128)(2,1)} %param.20) | copy-start | bytes 4718596
  38.9 0.9 copy-start.3
  43.9 13.1 %all-to-all-start.3 = ((f32[4,1,384]{2,1,0:T(1,128)}), f32[4,1,384]{2,1,0:T(1,128)S(1)}, u32[]{:S(2)}, u32[]{:S(2)}) async-start(f32[4,1,384]{2,1,0:T(1,128)} %reshape.484), calls=%async_computation.3 | async-start | bytes 12288 | tf_op jit(solution)/shard_map/all_to_all | solution.py:113
  49.8 12.2 %copy-start.4 = (f32[48,4,8,64]{3,2,1,0:T(8,128)S(1)}, f32[48,4,8,64]{3,2,1,0:T(8,128)}, u32[]{:S(2)}) copy-start(f32[48,4,8,64]{3,2,1,0:T(8,128)} %copy-done.3) | copy-start | bytes 1179652
  57.0 10.6 %all-to-all-start.2 = ((f32[4,1,384]{2,1,0:T(1,128)}), f32[4,1,384]{2,1,0:T(1,128)S(1)}, u32[]{:S(2)}, u32[]{:S(2)}) async-start(f32[4,1,384]{2,1,0:T(1,128)} %reshape.482), calls=%async_computation.2 | async-start | bytes 12288 | tf_op jit(solution)/shard_map/all_to_all | solution.py:112
  62.1 9.3 %copy-start.5 = (bf16[1,24,512]{2,1,0:T(8,128)(2,1)S(1)}, bf16[1,24,512]{2,1,0:T(8,128)(2,1)}, u32[]{:S(2)}) copy-start(bf16[1,24,512]{2,1,0:T(8,128)(2,1)} %param.17) | copy-start | bytes 73732
  62.1 9.3 %copy-start.6 = (bf16[1,24,512]{2,1,0:T(8,128)(2,1)S(1)}, bf16[1,24,512]{2,1,0:T(8,128)(2,1)}, u32[]{:S(2)}) copy-start(bf16[1,24,512]{2,1,0:T(8,128)(2,1)} %param.18) | copy-start | bytes 73732
  62.1 9.4 %copy-start.8 = (s32[24]{0:T(128)S(1)}, s32[24]{0:T(128)}, u32[]{:S(2)}) copy-start(s32[24]{0:T(128)} %get-tuple-element.6) | copy-start | bytes 292
  67.6 37.4 %all-to-all-start.1 = ((f32[1,4,12,4096]{3,0,2,1:T(1,128)}), f32[1,4,12,4096]{3,0,2,1:T(1,128)S(1)}, u32[]{:S(2)}, u32[]{:S(2)}) async-start(f32[1,4,12,4096]{3,0,2,1:T(1,128)} %bitcast.8), calls=%async_computation.1 | async-start | bytes 1572864 | tf_op jit(solution)/shard_map/all_to_all | solution.py:111
  106.4 120.3 %copy-start.10 = (f32[4096]{0:T(1024)S(1)}, f32[4096]{0:T(1024)}, u32[]{:S(2)}) copy-start(f32[4096]{0:T(1024)} %param.25) | copy-start | bytes 49156
  106.4 120.3 %copy-start.11 = (bf16[2048,2]{0,1:T(2,128)(2,1)S(1)}, bf16[2048,2]{0,1:T(2,128)(2,1)}, u32[]{:S(2)}) copy-start(bf16[2048,2]{0,1:T(2,128)(2,1)} %param.28) | copy-start | bytes 24580
  106.4 120.3 %copy-start.12 = (f32[2048]{0:T(1024)S(1)}, f32[2048]{0:T(1024)}, u32[]{:S(2)}) copy-start(f32[2048]{0:T(1024)} %param.27) | copy-start | bytes 24580
  111.5 134.2 %copy-start.9 = (f32[2]{0:T(128)S(1)}, f32[2]{0:T(128)}, u32[]{:S(2)}) copy-start(f32[2]{0:T(128)} %param.29) | copy-start | bytes 28
Sparse Core Ops, SparseCore 0:
  9.6 59.4 all-gather.2
  70.6 155.9 all-gather.4
where the time goes:
time: 254 us; the launch traced here: 253 us
  waiting for transfers between devices  150 us (59%)
  local copies, waits for them, and re-layouts  31.5 us (12%)
  matrix products  21.9 us (9%)
  starting transfers between devices  18.4 us (7%)
  between operations  14.4 us (6%)
  other arithmetic  12.3 us (5%)
  blocking collectives  4.94 us (2%)
    all_gather x1, waiting for transfers between devices, per_device(): lax.all_gather(head_weight, ('batch', 'section'), axis=0, tiled=True)  115 us
    all_to_all x1, waiting for transfers between devices, per_device(): lax.all_to_all(numerator, 'batch', split_axis=1, concat_axis=1, tiled=True)  27.7 us
    dot_general x1, matrix products, per_device(): jnp.dot(hidden, class_weight, preferred_element_type=jnp.float32)  14 us
    all_to_all x1, starting transfers between devices, per_device(): lax.all_to_all(outgoing_queries, 'batch', split_axis=1, concat_axis=1, ti...  6.35 us
    reshape x1, local copies, waits for them, and re-layouts, per_device(): key_pages[:, served_pages].reshape(batch_rows, context, kv_local, HD)  5.62 us
    reshape x1, local copies, waits for them, and re-layouts, per_device(): value_pages[:, served_pages].reshape(batch_rows, context, kv_local, HD)  5.6 us
  transfers between devices with their start and end apart: 6, of which 4 were waited for; matrix products, arithmetic and copies ran while one was open for 20% of the time, Pallas kernels for 0%

commit v1 on v0

v1 whole, which is shorter than its diff:
```python
import functools

import jax
import jax.numpy as jnp
from jax import lax
from jax.experimental import pallas as pl
from jax.experimental.pallas import tpu as pltpu
from jax.sharding import PartitionSpec as P

HD = 128
MESH = pl.DeviceIdType.MESH


def fused_kernel(
    dims,
    table_ref,
    class_bias_ref,
    mail_ref,
    keys_hbm,
    values_hbm,
    rows_hbm,
    gain_ref,
    weight_hbm,
    bias_ref,
    class_ref,
    attention_ref,
    odds_ref,
    mail_in,
    served_out,
    returned,
    keys,
    values,
    raw,
    normed,
    weights,
    total,
    partial,
    logits_in,
    local_sem,
    mail_send,
    mail_recv,
    back_send,
    back_recv,
    line_send,
    line_recv,
    twin_send,
    twin_recv,
    swap_send,
    swap_recv,
    row_send,
    row_recv,
    norm_send,
    norm_recv,
    sum_send,
    sum_recv,
):
    nb, ng, mp, ns = dims["nb"], dims["ng"], dims["mp"], dims["ns"]
    cap, page_count, kvl, group = dims["cap"], dims["page_count"], dims["kvl"], dims["group"]
    half, chunk, chunks, depth = dims["half"], dims["chunk"], dims["chunks"], dims["depth"]
    row_chunks = dims["row_chunks"]
    slots = attention_ref.shape[0]
    heads = kvl * group
    z, y = lax.axis_index("batch"), lax.axis_index("group")
    x, c = lax.axis_index("mp"), lax.axis_index("section")
    other = 1 - c
    twin = 1 - y
    cross = lax.rem(c + y, 2)
    row_count, row_width = rows_hbm.shape
    per_chunk = row_count // row_chunks

    def remote(src, dst, send, recv, device):
        return pltpu.make_async_remote_copy(
            src_ref=src, dst_ref=dst, send_sem=send, recv_sem=recv, device_id=device, device_id_type=MESH
        )

    def columns(owner, n):
        return pl.ds(pl.multiple_of(owner * half + n * chunk, chunk), chunk)

    barrier = pltpu.get_barrier_semaphore()

    def greet(device):
        pl.semaphore_signal(barrier, inc=1, device_id=device, device_id_type=MESH)

    for d in range(1, nb):
        greet({"batch": lax.rem(z + d, nb)})

    @pl.when(z > 0)
    def _():
        greet({"batch": z - 1, "section": other})

    @pl.when(z < nb - 1)
    def _():
        greet({"batch": z + 1, "section": other})

    greet({"section": other})
    greet({"group": twin})
    for d in range(1, mp):
        peer = lax.rem(x + d, mp)
        greet({"mp": peer})
        greet({"mp": peer, "section": other})
    neighbours = jnp.where(z > 0, 1, 0) + jnp.where(z < nb - 1, 1, 0)
    pl.semaphore_wait(barrier, (nb - 1) + 2 + 2 * (mp - 1) + neighbours)

    def mail(d):
        target = lax.rem(z + d, nb)
        return remote(mail_ref.at[target], mail_in.at[z], mail_send.at[d], mail_recv.at[d], {"batch": target})

    def back(d):
        target = lax.rem(z + d, nb)
        return remote(
            served_out.at[target], returned.at[z], back_send.at[d], back_recv.at[d], {"batch": target}
        )

    def row_copy(d, i):
        target = lax.rem(x + d, mp)
        part = pl.ds(i * per_chunk, per_chunk)
        return remote(
            rows_hbm.at[part], raw.at[x, part], row_send.at[d, i], row_recv.at[d, i], {"mp": target}
        )

    def swap(n):
        return remote(
            weight_hbm.at[:, columns(other, n)],
            weights.at[z, c, n],
            swap_send.at[n],
            swap_recv.at[n],
            {"section": other},
        )

    def first_hop(direction, n):
        return remote(
            weight_hbm.at[:, columns(cross, n)],
            weights.at[z, c, n],
            line_send.at[direction, 0, n],
            line_recv.at[direction, 0, n],
            {"batch": z + (1 if direction == 0 else -1), "section": cross},
        )

    def later_hop(direction, hop, n, piece):
        return remote(
            weights.at[piece, cross, n],
            weights.at[piece, cross, n],
            line_send.at[direction, hop, n],
            line_recv.at[direction, hop, n],
            {"batch": z + (1 if direction == 0 else -1)},
        )

    def twin_copy(piece, n, kind):
        return remote(
            weights.at[piece, kind, n],
            weights.at[piece, kind, n],
            twin_send.at[piece, n],
            twin_recv.at[piece, n],
            {"group": twin},
        )

    def norm_copy(i):
        part = pl.ds(i * per_chunk, per_chunk)
        return remote(
            normed.at[c, :, part],
            normed.at[c, :, part],
            norm_send.at[i],
            norm_recv.at[i],
            {"section": other},
        )

    def sum_copy(d, e):
        peer, side = lax.rem(x + d, mp), lax.rem(c + e, 2)
        return remote(
            partial.at[side],
            logits_in.at[d * 2 + e],
            sum_send.at[d * 2 + e],
            sum_recv.at[d * 2 + e],
            {"mp": peer, "section": side},
        )

    own_copies = [
        pltpu.make_async_copy(keys_hbm.at[0], keys, local_sem.at[0]),
        pltpu.make_async_copy(values_hbm.at[0], values, local_sem.at[1]),
        pltpu.make_async_copy(mail_ref.at[z], mail_in.at[z], local_sem.at[2]),
        pltpu.make_async_copy(rows_hbm, raw.at[x], local_sem.at[3]),
    ]
    own_weights = [
        pltpu.make_async_copy(weight_hbm.at[:, columns(c, n)], weights.at[z, c, n], local_sem.at[5 + n])
        for n in range(chunks)
    ]

    for d in range(1, nb):
        mail(d).start()
    for n in range(chunks):

        @pl.when(z < nb - 1)
        def _():
            first_hop(0, n).start()

        @pl.when(z > 0)
        def _():
            first_hop(1, n).start()

    for i in range(row_chunks):
        for d in range(1, mp):
            row_copy(d, i).start()
    for copy in own_copies:
        copy.start()
    for n in range(chunks):
        swap(n).start()
    for copy in own_weights:
        copy.start()

    for side in range(2):
        total[side] = jnp.broadcast_to(
            bias_ref[:, pl.ds(pl.multiple_of(c * half, half), half)], total.shape[1:]
        )

    for copy in own_copies[:3]:
        copy.wait()
    for d in range(1, nb):
        mail(d).wait_recv()

    scale = 1.0 / HD**0.5
    context = page_count * keys.shape[1]
    head_of_row = lax.broadcasted_iota(jnp.int32, (heads, HD), 0) // group
    position = lax.broadcasted_iota(jnp.int32, (heads, context), 1)
    step = 4 if cap % 4 == 0 else cap
    blocks = cap // step

    def serve(d, r):
        base = (d * cap + r) * (page_count + 1)
        pages = [table_ref[base + i] for i in range(page_count)]
        length = table_ref[base + page_count]
        key_block = jnp.concatenate([keys[p] for p in pages], axis=0)
        value_block = jnp.concatenate([values[p] for p in pages], axis=0)
        letter = mail_in[d, r]
        query = letter[:heads]
        own_key = letter[heads : heads + kvl].astype(jnp.float32)
        own_value = letter[heads + kvl : heads + 2 * kvl].astype(jnp.float32)
        zero = jnp.zeros_like(query)
        wide = jnp.concatenate([jnp.where(head_of_row == h, query, zero) for h in range(kvl)], axis=1)
        scores = (
            lax.dot_general(
                wide, key_block, (((1,), (1,)), ((), ())), preferred_element_type=jnp.float32
            )
            * scale
        )
        scores = jnp.where(position < length, scores, -1e30)
        top = jnp.max(scores, axis=1, keepdims=True)
        w = jnp.exp(scores - top)
        den = jnp.sum(w, axis=1, keepdims=True)
        everything = jnp.dot(w.astype(jnp.bfloat16), value_block, preferred_element_type=jnp.float32)
        num = jnp.zeros((heads, HD), jnp.float32)
        key_rows = jnp.zeros((heads, HD), jnp.float32)
        value_rows = jnp.zeros((heads, HD), jnp.float32)
        for h in range(kvl):
            here = head_of_row == h
            num = jnp.where(here, everything[:, h * HD : (h + 1) * HD], num)
            key_rows = jnp.where(here, own_key[h : h + 1], key_rows)
            value_rows = jnp.where(here, own_value[h : h + 1], value_rows)
        own_score = jnp.sum(query.astype(jnp.float32) * key_rows, axis=1, keepdims=True) * scale
        own = jnp.exp(own_score - top)
        return ((num + own * value_rows) / (den + own)).astype(jnp.bfloat16)

    def serve_block(index, carry):
        d, r0 = index // blocks, lax.rem(index, blocks) * step
        results = [serve(d, r0 + u) for u in range(step)]
        for u in range(step):
            served_out[d, r0 + u] = results[u]
        return carry

    lax.fori_loop(0, nb * blocks, serve_block, 0)
    for d in range(1, nb):
        back(d).start()
    own_back = pltpu.make_async_copy(served_out.at[z], returned.at[z], local_sem.at[4])
    own_back.start()

    def line_step(r, n):
        @pl.when(z - r >= 0)
        def _():
            piece = z - r
            later_hop(0, r - 1, n, piece).wait_recv()

            @pl.when(z + 1 < nb)
            def _():
                later_hop(0, r, n, piece).start()

            twin_copy(piece, n, cross).start()

        @pl.when(z + r < nb)
        def _():
            piece = z + r
            later_hop(1, r - 1, n, piece).wait_recv()

            @pl.when(z > 0)
            def _():
                later_hop(1, r, n, piece).start()

            twin_copy(piece, n, cross).start()

    features = row_width * mp
    pieces_per_block = row_width // depth
    fine = min(16, per_chunk)

    def row_step(i):
        for d in range(1, mp):
            row_copy(d, i).wait_recv()

        def normalise(j, carry):
            start = pl.multiple_of(i * per_chunk + j * fine, fine)
            part = pl.ds(start, fine)
            power = jnp.zeros((fine, 1), jnp.float32)
            for b in range(mp):
                block = raw[b, part].astype(jnp.float32)
                power = power + jnp.sum(block * block, axis=1, keepdims=True)
            factor = lax.rsqrt(power / features + 1e-06)
            for b in range(mp):
                block = raw[b, part].astype(jnp.float32)
                gain = gain_ref[:, b * row_width : (b + 1) * row_width]
                result = (block * factor * gain).astype(jnp.bfloat16)
                for p in range(pieces_per_block):
                    normed[c, b * pieces_per_block + p, part] = result[:, p * depth : (p + 1) * depth]
            return carry

        lax.fori_loop(0, per_chunk // fine, normalise, 0)
        norm_copy(i).start()

    own_copies[3].wait()
    early = [(r, n) for r in range(1, nb - 1) for n in range(chunks)]
    for i in range(row_chunks):
        for r, n in early[len(early) * i // row_chunks : len(early) * (i + 1) // row_chunks]:
            line_step(r, n)
        row_step(i)
    for i in range(row_chunks):
        norm_copy(i).wait_recv()

    def multiply(piece, kind, n):
        for side in range(2):
            total[side, :, n * chunk : (n + 1) * chunk] += jnp.dot(
                normed[side, piece * ns + kind], weights[piece, kind, n], preferred_element_type=jnp.float32
            )

    def multiply_own(n):
        own_weights[n].wait()
        swap(n).wait_recv()
        multiply(z, 0, n)
        multiply(z, 1, n)

    def multiply_at(r, n):
        def both(piece):
            multiply(piece, cross, n)
            twin_copy(piece, n, 1 - cross).wait_recv()
            multiply(piece, 1 - cross, n)

        def left():
            both(z - r)

        def right():
            both(z + r)

        pl.when(z - r >= 0)(left)
        pl.when(z + r < nb)(right)

    for n in range(chunks):
        multiply_own(n)

        def near(r, carry):
            multiply_at(r, n)
            return carry

        lax.fori_loop(1, nb - 1, near, 0)
        line_step(nb - 1, n)

    for n in range(chunks):
        multiply_at(nb - 1, n)

    class_part = class_ref[:, pl.ds(pl.multiple_of(c * half, half), half)]
    for side in range(2):
        hidden = jnp.maximum(total[side], 0.0).astype(jnp.bfloat16)
        partial[side] = lax.dot_general(
            class_part, hidden, (((1,), (1,)), ((), ())), preferred_element_type=jnp.float32
        )
    pairs = [(d, e) for d in range(mp) for e in range(2) if d or e]
    for d, e in pairs:
        sum_copy(d, e).start()

    own_back.wait()
    for d in range(1, nb):
        back(d).wait_recv()
    pick = nb * cap * (page_count + 1)

    def place(j, carry):
        attention_ref[j] = returned[table_ref[pick + j], table_ref[pick + slots + j]]
        return carry

    lax.fori_loop(0, slots, place, 0)

    logits = partial[c]
    for d, e in pairs:
        sum_copy(d, e).wait_recv()
        logits = logits + logits_in[d * 2 + e]
    odds_ref[...] = (logits[1:2] + class_bias_ref[1]) - (logits[0:1] + class_bias_ref[0])

    for d in range(1, nb):
        mail(d).wait_send()
        back(d).wait_send()
    for i in range(row_chunks):
        for d in range(1, mp):
            row_copy(d, i).wait_send()
        norm_copy(i).wait_send()
    for d, e in pairs:
        sum_copy(d, e).wait_send()
    for n in range(chunks):
        swap(n).wait_send()

        @pl.when(z < nb - 1)
        def _():
            first_hop(0, n).wait_send()

        @pl.when(z > 0)
        def _():
            first_hop(1, n).wait_send()

        def drain(r, carry):
            @pl.when(z - r >= 0)
            def _():
                @pl.when(z + 1 < nb)
                def _():
                    later_hop(0, r, n, z - r).wait_send()

                twin_copy(z - r, n, cross).wait_send()

            @pl.when(z + r < nb)
            def _():
                @pl.when(z > 0)
                def _():
                    later_hop(1, r, n, z + r).wait_send()

                twin_copy(z + r, n, cross).wait_send()

            return carry

        lax.fori_loop(1, nb, drain, 0)


def per_device(
    queries,
    new_keys,
    new_values,
    key_pages,
    value_pages,
    page_table,
    ancestry,
    lengths,
    step_rows,
    norm_gain,
    head_weight,
    head_bias,
    class_weight,
    class_bias,
):
    slot_count, page_count = page_table.shape
    kv_width = key_pages.shape[3]
    kvl = kv_width // HD
    group = queries.shape[2] // kv_width
    heads = kvl * group
    nb, ng = lax.axis_size("batch"), lax.axis_size("group")
    mp, ns = lax.axis_size("mp"), lax.axis_size("section")
    assert ng == 2 and ns == 2 and queries.shape[0] == 1
    z = lax.axis_index("batch")
    cap = max(2, (2 * slot_count + nb - 1) // nb)

    source = (ancestry // slot_count).reshape(nb, slot_count)
    positions = jnp.arange(slot_count)
    earlier = positions[None, :] < positions[:, None]
    same_source = source[:, :, None] == source[:, None, :]
    rank = jnp.sum(same_source & earlier[None, :, :], axis=2)
    slot_ids = jnp.arange(cap)
    served = (source == z)[:, None, :] & (rank[:, None, :] == slot_ids[None, :, None])
    served_slot = jnp.sum(jnp.where(served, positions[None, None, :], 0), axis=2)
    own_source = lax.dynamic_index_in_dim(source, z, 0, keepdims=False)
    own_rank = lax.dynamic_index_in_dim(rank, z, 0, keepdims=False)
    local_lengths = lax.dynamic_slice_in_dim(lengths, z * slot_count, slot_count)
    facts = jnp.concatenate([page_table, local_lengths[:, None]], axis=1)
    table = jnp.concatenate([facts[served_slot].reshape(-1), own_source, own_rank])
    wanted = (own_source[None, None, :] == jnp.arange(nb)[:, None, None]) & (
        own_rank[None, None, :] == slot_ids[None, :, None]
    )
    request_slot = jnp.sum(jnp.where(wanted, positions[None, None, :], 0), axis=2)
    letters = jnp.concatenate([queries[0], new_keys[0], new_values[0]], axis=1)
    lines = heads + 2 * kvl
    mail = jnp.take(letters, request_slot.reshape(-1), axis=0).reshape(nb, cap, lines, HD)

    row_count, row_width = step_rows.shape
    depth, width = head_weight.shape
    half = width // ns
    chunk = min(256, half)
    chunks = half // chunk
    row_chunks = 4
    pieces = nb * ns
    dims = dict(
        nb=nb, ng=ng, mp=mp, ns=ns, cap=cap, page_count=page_count, kvl=kvl, group=group,
        half=half, chunk=chunk, chunks=chunks, depth=depth, row_chunks=row_chunks,
    )
    class_rows = jnp.zeros((8, width), class_weight.dtype).at[:2].set(class_weight.T)
    smem = pl.BlockSpec(memory_space=pltpu.SMEM)
    vmem = pl.BlockSpec(memory_space=pltpu.VMEM)
    anywhere = pl.BlockSpec(memory_space=pl.ANY)
    bf16, f32 = jnp.bfloat16, jnp.float32
    sems = pltpu.SemaphoreType.DMA
    attention, odds = pl.pallas_call(
        functools.partial(fused_kernel, dims),
        out_shape=(
            jax.ShapeDtypeStruct((slot_count, heads, HD), bf16),
            jax.ShapeDtypeStruct((1, row_count), f32),
        ),
        in_specs=[smem, smem, vmem, anywhere, anywhere, anywhere, vmem, anywhere, vmem, vmem],
        out_specs=(vmem, vmem),
        scratch_shapes=[
            pltpu.VMEM((nb, cap, lines, HD), bf16),
            pltpu.VMEM((nb, cap, heads, HD), bf16),
            pltpu.VMEM((nb, cap, heads, HD), bf16),
            pltpu.VMEM(key_pages.shape[1:], bf16),
            pltpu.VMEM(key_pages.shape[1:], bf16),
            pltpu.VMEM((mp, row_count, row_width), bf16),
            pltpu.VMEM((2, pieces, row_count, depth), bf16),
            pltpu.VMEM((nb, ns, chunks, depth, chunk), bf16),
            pltpu.VMEM((2, row_count, half), f32),
            pltpu.VMEM((2, 8, row_count), f32),
            pltpu.VMEM((2 * mp, 8, row_count), f32),
            sems((5 + chunks,)),
            sems((nb,)),
            sems((nb,)),
            sems((nb,)),
            sems((nb,)),
            sems((2, nb, chunks)),
            sems((2, nb, chunks)),
            sems((nb, chunks)),
            sems((nb, chunks)),
            sems((chunks,)),
            sems((chunks,)),
            sems((mp, row_chunks)),
            sems((mp, row_chunks)),
            sems((row_chunks,)),
            sems((row_chunks,)),
            sems((2 * mp,)),
            sems((2 * mp,)),
        ],
        compiler_params=pltpu.CompilerParams(
            collective_id=0, has_side_effects=True, vmem_limit_bytes=60 * 1024 * 1024
        ),
        name="filter_round",
    )(
        table,
        class_bias,
        mail,
        key_pages,
        value_pages,
        step_rows,
        norm_gain.reshape(1, -1),
        head_weight,
        head_bias.reshape(1, -1),
        class_rows,
    )
    return attention.reshape(1, slot_count, heads * HD), odds.reshape(-1)


def solution(mesh):
    placed = (
        P("section", ("group", "batch"), "mp"),
        P("section", ("group", "batch"), "mp"),
        P("section", ("group", "batch"), "mp"),
        P("section", ("group", "batch"), None, "mp"),
        P("section", ("group", "batch"), None, "mp"),
        P(("group", "batch"), None),
        P("group"),
        P("group"),
        P(("group", "batch", "section"), "mp"),
        P(),
        P(("batch", "section"), "mp"),
        P("mp"),
        P("mp", None),
        P(),
    )
    return jax.shard_map(
        per_device,
        mesh=mesh,
        in_specs=placed,
        out_specs=(P("section", ("group", "batch"), "mp"), P(("group", "batch", "section"))),
        check_vma=False,
    )
```

time: 254 us -> 118 us (0.46)
  waiting for transfers between devices: 150 us -> 0 us
  Pallas kernels: 0 us -> 106 us
  local copies, waits for them, and re-layouts: 31.5 us -> 5.89 us
  matrix products: 21.9 us -> 0 us
  starting transfers between devices: 18.4 us -> 0 us
  between operations: 14.4 us -> 0.74 us
  other arithmetic: 12.3 us -> 4.74 us
  blocking collectives: 4.94 us -> 0 us
    all_gather x2 -> x0, waiting for transfers between devices: 115 us -> none  [the longest x1 115 us: per_device(): lax.all_gather(head_weight, ('batch', 'section'), axis=0, tiled=True)]
    pallas_call x0 -> x1, Pallas kernels: none -> 106 us  [per_device(): pl.pallas_call(functools.partial(fused_kernel, dims), out_shape=(jax.Shap...]
    all_to_all x4 -> x0, waiting for transfers between devices: 33.1 us -> none  [the longest x1 27.7 us: per_device(): lax.all_to_all(numerator, 'batch', split_axis=1, concat_axis=1, tiled=True)]
    dot_general x4 -> x0, matrix products: 21.9 us -> none  [the longest x1 14 us: per_device(): jnp.dot(hidden, class_weight, preferred_element_type=jnp.float32)]
    all_to_all x4 -> x0, starting transfers between devices: 18.3 us -> none  [the longest x1 6.35 us: per_device(): lax.all_to_all(outgoing_queries, 'batch', split_axis=1, concat_axis=1, ti...]
    reshape x7 -> x4, local copies, waits for them, and re-layouts: 14.3 us -> 1.98 us  [the longest x1 1.69 us: per_device(): return (attention.reshape(1, slot_count, heads * HD), odds.reshape(-1))]
    gather x12 -> x2, local copies, waits for them, and re-layouts: 11.5 us -> 1.43 us  [the longest x1 0.83 us: per_device(): jnp.take(letters, request_slot.reshape(-1), axis=0)]
    psum x1 -> x0, blocking collectives: 4.94 us -> none  [per_device(): logits = lax.psum(partial_logits, 'mp') + class_bias]
  transfers between devices with their start and end apart: 6 -> 0, of which waited for: 4 -> 0; matrix products, arithmetic and copies ran while one was open for 20% -> 0% of each run, Pallas kernels for 0% -> 0%
where the time goes in v1:
time: 118 us; the launch traced here: 117 us
  Pallas kernels  106 us (90%)
  local copies, waits for them, and re-layouts  5.89 us (5%)
  other arithmetic  4.74 us (4%)
    pallas_call x1, Pallas kernels, per_device(): pl.pallas_call(functools.partial(fused_kernel, dims), out_shape=(jax.Shap...  106 us

profile of v1, /device:TPU:0, one launch (start us, length us, event | category | flops | bytes accessed | tf_op | source)
XLA Modules:
  0.0 117.2 jit_solution(5185584073469689504)
XLA Ops:
  0.6 0.0 copy-start
  0.6 0.7 and_select_fusion
  1.3 0.1 reshape.173
  1.4 0.2 convert_reduce_fusion
  1.6 0.0 copy-done
  1.7 0.1 dynamic-slice_bitcast_fusion.2
  1.7 0.7 pad_add_fusion
  2.4 0.1 copy.22
  2.5 0.3 select_reduce_fusion.1
  2.8 0.1 copy.21
  2.9 0.1 reshape.182
  3.0 0.6 gather_fusion
  3.6 0.1 reshape.174
  3.7 0.7 pad_add_fusion.1.table_ref
  4.4 1.0 pad_maximum_fusion
  5.4 0.3 select_reduce_fusion
  5.7 0.1 copy.24
  5.8 0.1 reshape.175
  5.9 0.0 copy-start.1
  5.9 0.8 gather_fusion.1
  6.7 0.1 copy.25
  6.8 0.1 copy.23
  6.9 0.9 broadcast_select_fusion.mail_ref
  7.8 0.0 copy-done.1
  7.8 0.6 scatter.4.class_ref
  8.4 105.8 %filter_round.1 = (bf16[24,32,128]{2,1,0:T(8,128)(2,1)}, f32[1,512]{1,0:T(1,128)}) custom-call(s32[288]{0:T(512)} %pad_add_fusion.1.table_ref, f32[2]{0:T(128)} %class_bias_ref.1, bf16[4,12,40,128]{3,2,1,0:T(8,128)(2,1)} %broadcast_select_fusion.mail_ref, bf16[1,96,16,512]{3,2,1,0:T(8,128)(2,1)} %keys_hbm.1, bf16[1,96,16,512]{3,2,1,0:T(8,128)(2,1)} %values_hbm.1, ...), custom_call_target="tpu_custom_call" | custom-call | tf_op jit(solution)/shard_map/filter_round/pallas_call | solution.py:508
  114.2 1.7 %reshape.178 = bf16[1,24,4096]{2,1,0:T(8,128)(2,1)} reshape(bf16[24,32,128]{2,1,0:T(8,128)(2,1)} %get-tuple-element.16) | data formatting | bytes 393216 | tf_op jit(solution)/shard_map/reshape | solution.py:562
  115.9 1.2 %copy.27 = f32[512]{0:T(512)} copy(f32[512]{0:T(512)} %bitcast.30) | data formatting | bytes 4096
  (10 shorter events, 0.1 us)
Async XLA Ops:
  0.6 1.0 copy-start
  5.9 1.9 %copy-start.1 = (bf16[2048,2]{0,1:T(2,128)(2,1)S(1)}, bf16[2048,2]{0,1:T(2,128)(2,1)}, u32[]{:S(2)}) copy-start(bf16[2048,2]{0,1:T(2,128)(2,1)} %param.28) | copy-start | bytes 24580

commit v2 on v1

--- a/solution.py
+++ b/solution.py
@@ -36,6 +36,7 @@
     total,
     partial,
     logits_in,
+    gathered,
     local_sem,
     mail_send,
     mail_recv,
@@ -127,30 +128,36 @@
             {"section": other},
         )
 
-    def first_hop(direction, n):
-        return remote(
-            weight_hbm.at[:, columns(cross, n)],
-            weights.at[z, c, n],
-            line_send.at[direction, 0, n],
-            line_recv.at[direction, 0, n],
+    parts = 2 * chunks
+    sub = depth // 2
+
+    def lines(q):
+        return pl.ds((q % 2) * sub, sub)
+
+    def first_hop(direction, q):
+        return remote(
+            weight_hbm.at[lines(q), columns(cross, q // 2)],
+            weights.at[z, c, q // 2, lines(q)],
+            line_send.at[direction, 0, q],
+            line_recv.at[direction, 0, q],
             {"batch": z + (1 if direction == 0 else -1), "section": cross},
         )
 
-    def later_hop(direction, hop, n, piece):
-        return remote(
-            weights.at[piece, cross, n],
-            weights.at[piece, cross, n],
-            line_send.at[direction, hop, n],
-            line_recv.at[direction, hop, n],
+    def later_hop(direction, hop, q, piece):
+        return remote(
+            weights.at[piece, cross, q // 2, lines(q)],
+            weights.at[piece, cross, q // 2, lines(q)],
+            line_send.at[direction, hop, q],
+            line_recv.at[direction, hop, q],
             {"batch": z + (1 if direction == 0 else -1)},
         )
 
-    def twin_copy(piece, n, kind):
-        return remote(
-            weights.at[piece, kind, n],
-            weights.at[piece, kind, n],
-            twin_send.at[piece, n],
-            twin_recv.at[piece, n],
+    def twin_copy(piece, q, kind):
+        return remote(
+            weights.at[piece, kind, q // 2, lines(q)],
+            weights.at[piece, kind, q // 2, lines(q)],
+            twin_send.at[piece, q],
+            twin_recv.at[piece, q],
             {"group": twin},
         )
 
@@ -187,15 +194,15 @@
 
     for d in range(1, nb):
         mail(d).start()
-    for n in range(chunks):
+    for q in range(parts):
 
         @pl.when(z < nb - 1)
         def _():
-            first_hop(0, n).start()
+            first_hop(0, q).start()
 
         @pl.when(z > 0)
         def _():
-            first_hop(1, n).start()
+            first_hop(1, q).start()
 
     for i in range(row_chunks):
         for d in range(1, mp):
@@ -272,28 +279,28 @@
     own_back = pltpu.make_async_copy(served_out.at[z], returned.at[z], local_sem.at[4])
     own_back.start()
 
-    def line_step(r, n):
+    def line_step(r, q):
         @pl.when(z - r >= 0)
         def _():
             piece = z - r
-            later_hop(0, r - 1, n, piece).wait_recv()
+            later_hop(0, r - 1, q, piece).wait_recv()
 
             @pl.when(z + 1 < nb)
             def _():
-                later_hop(0, r, n, piece).start()
-
-            twin_copy(piece, n, cross).start()
+                later_hop(0, r, q, piece).start()
+
+            twin_copy(piece, q, cross).start()
 
         @pl.when(z + r < nb)
         def _():
             piece = z + r
-            later_hop(1, r - 1, n, piece).wait_recv()
+            later_hop(1, r - 1, q, piece).wait_recv()
 
             @pl.when(z > 0)
             def _():
-                later_hop(1, r, n, piece).start()
-
-            twin_copy(piece, n, cross).start()
+                later_hop(1, r, q, piece).start()
+
+            twin_copy(piece, q, cross).start()
 
     features = row_width * mp
     pieces_per_block = row_width // depth
@@ -323,10 +330,10 @@
         norm_copy(i).start()
 
     own_copies[3].wait()
-    early = [(r, n) for r in range(1, nb - 1) for n in range(chunks)]
+    early = [(r, q) for r in range(1, nb - 1) for q in range(parts)]
     for i in range(row_chunks):
-        for r, n in early[len(early) * i // row_chunks : len(early) * (i + 1) // row_chunks]:
-            line_step(r, n)
+        for r, q in early[len(early) * i // row_chunks : len(early) * (i + 1) // row_chunks]:
+            line_step(r, q)
         row_step(i)
     for i in range(row_chunks):
         norm_copy(i).wait_recv()
@@ -346,7 +353,8 @@
     def multiply_at(r, n):
         def both(piece):
             multiply(piece, cross, n)
-            twin_copy(piece, n, 1 - cross).wait_recv()
+            twin_copy(piece, 2 * n, 1 - cross).wait_recv()
+            twin_copy(piece, 2 * n + 1, 1 - cross).wait_recv()
             multiply(piece, 1 - cross, n)
 
         def left():
@@ -357,6 +365,20 @@
 
         pl.when(z - r >= 0)(left)
         pl.when(z + r < nb)(right)
+
+    def place_attention():
+        own_back.wait()
+        for d in range(1, nb):
+            back(d).wait_recv()
+        pick = nb * cap * (page_count + 1)
+
+        def place(j, carry):
+            gathered[j] = returned[table_ref[pick + j], table_ref[pick + slots + j]].astype(jnp.float32)
+            return carry
+
+        lax.fori_loop(0, slots, place, 0)
+        for h in range(heads):
+            attention_ref[:, h * HD : (h + 1) * HD] = gathered[:, h, :].astype(jnp.bfloat16)
 
     for n in range(chunks):
         multiply_own(n)
@@ -366,10 +388,16 @@
             return carry
 
         lax.fori_loop(1, nb - 1, near, 0)
-        line_step(nb - 1, n)
-
-    for n in range(chunks):
-        multiply_at(nb - 1, n)
+        line_step(nb - 1, 2 * n)
+        line_step(nb - 1, 2 * n + 1)
+        if n > 0:
+            multiply_at(nb - 1, n - 1)
+        if n == chunks - 2:
+            place_attention()
+
+    if chunks == 1:
+        place_attention()
+    multiply_at(nb - 1, chunks - 1)
 
     class_part = class_ref[:, pl.ds(pl.multiple_of(c * half, half), half)]
     for side in range(2):
@@ -380,17 +408,6 @@
     pairs = [(d, e) for d in range(mp) for e in range(2) if d or e]
     for d, e in pairs:
         sum_copy(d, e).start()
-
-    own_back.wait()
-    for d in range(1, nb):
-        back(d).wait_recv()
-    pick = nb * cap * (page_count + 1)
-
-    def place(j, carry):
-        attention_ref[j] = returned[table_ref[pick + j], table_ref[pick + slots + j]]
-        return carry
-
-    lax.fori_loop(0, slots, place, 0)
 
     logits = partial[c]
     for d, e in pairs:
@@ -409,31 +426,32 @@
         sum_copy(d, e).wait_send()
     for n in range(chunks):
         swap(n).wait_send()
+    for q in range(parts):
 
         @pl.when(z < nb - 1)
         def _():
-            first_hop(0, n).wait_send()
+            first_hop(0, q).wait_send()
 
         @pl.when(z > 0)
         def _():
-            first_hop(1, n).wait_send()
+            first_hop(1, q).wait_send()
 
         def drain(r, carry):
             @pl.when(z - r >= 0)
             def _():
                 @pl.when(z + 1 < nb)
                 def _():
-                    later_hop(0, r, n, z - r).wait_send()
-
-                twin_copy(z - r, n, cross).wait_send()
+                    later_hop(0, r, q, z - r).wait_send()
+
+                twin_copy(z - r, q, cross).wait_send()
 
             @pl.when(z + r < nb)
             def _():
                 @pl.when(z > 0)
                 def _():
-                    later_hop(1, r, n, z + r).wait_send()
-
-                twin_copy(z + r, n, cross).wait_send()
+                    later_hop(1, r, q, z + r).wait_send()
+
+                twin_copy(z + r, q, cross).wait_send()
 
             return carry
 
@@ -479,14 +497,14 @@
     own_rank = lax.dynamic_index_in_dim(rank, z, 0, keepdims=False)
     local_lengths = lax.dynamic_slice_in_dim(lengths, z * slot_count, slot_count)
     facts = jnp.concatenate([page_table, local_lengths[:, None]], axis=1)
-    table = jnp.concatenate([facts[served_slot].reshape(-1), own_source, own_rank])
+    table = jnp.concatenate([facts.at[served_slot.reshape(-1)].get(mode="promise_in_bounds").reshape(-1), own_source, own_rank])
     wanted = (own_source[None, None, :] == jnp.arange(nb)[:, None, None]) & (
         own_rank[None, None, :] == slot_ids[None, :, None]
     )
     request_slot = jnp.sum(jnp.where(wanted, positions[None, None, :], 0), axis=2)
     letters = jnp.concatenate([queries[0], new_keys[0], new_values[0]], axis=1)
     lines = heads + 2 * kvl
-    mail = jnp.take(letters, request_slot.reshape(-1), axis=0).reshape(nb, cap, lines, HD)
+    mail = letters.at[request_slot.reshape(-1)].get(mode="promise_in_bounds").reshape(nb, cap, lines, HD)
 
     row_count, row_width = step_rows.shape
     depth, width = head_weight.shape
@@ -508,7 +526,7 @@
     attention, odds = pl.pallas_call(
         functools.partial(fused_kernel, dims),
         out_shape=(
-            jax.ShapeDtypeStruct((slot_count, heads, HD), bf16),
+            jax.ShapeDtypeStruct((slot_count, heads * HD), bf16),
             jax.ShapeDtypeStruct((1, row_count), f32),
         ),
         in_specs=[smem, smem, vmem, anywhere, anywhere, anywhere, vmem, anywhere, vmem, vmem],
@@ -525,15 +543,16 @@
             pltpu.VMEM((2, row_count, half), f32),
             pltpu.VMEM((2, 8, row_count), f32),
             pltpu.VMEM((2 * mp, 8, row_count), f32),
+            pltpu.VMEM((slot_count, heads, HD), f32),
             sems((5 + chunks,)),
             sems((nb,)),
             sems((nb,)),
             sems((nb,)),
             sems((nb,)),
-            sems((2, nb, chunks)),
-            sems((2, nb, chunks)),
-            sems((nb, chunks)),
-            sems((nb, chunks)),
+            sems((2, nb, 2 * chunks)),
+            sems((2, nb, 2 * chunks)),
+            sems((nb, 2 * chunks)),
+            sems((nb, 2 * chunks)),
             sems((chunks,)),
             sems((chunks,)),
             sems((mp, row_chunks)),
@@ -559,7 +578,7 @@
         head_bias.reshape(1, -1),
         class_rows,
     )
-    return attention.reshape(1, slot_count, heads * HD), odds.reshape(-1)
+    return attention[None], odds.reshape(-1)
 
 
 def solution(mesh):

time: 118 us -> 119 us (level)
    unnamed x6 -> x7, local copies, waits for them, and re-layouts: 1.32 us -> 3.71 us
    reshape x2, local copies, waits for them, and re-layouts: 1.81 us -> 0.2 us  [the longest x1 0.12 us: per_device(): facts.at[served_slot.reshape(-1)].get(mode='promise_in_bounds').reshape(-1)]
where the time goes in v2:
time: 119 us; the launch traced here: 118 us
  Pallas kernels  107 us (90%)
  local copies, waits for them, and re-layouts  6.49 us (5%)
  other arithmetic  3.83 us (3%)
    pallas_call x1, Pallas kernels, per_device(): pl.pallas_call(functools.partial(fused_kernel, dims), out_shape=(jax.Shap...  107 us
    unnamed x7, local copies, waits for them, and re-layouts  3.71 us

profile of v2, /device:TPU:0, one launch (start us, length us, event | category | flops | bytes accessed | tf_op | source)
XLA Modules:
  0.0 117.9 jit_solution(11423899097009589462)
XLA Ops:
  0.6 0.0 copy-start
  0.6 0.7 and_select_fusion
  1.3 0.1 reshape.179
  1.4 0.2 convert_reduce_fusion
  1.7 0.3 select_reduce_fusion
  2.0 0.1 copy.23
  2.1 0.1 reshape.182
  2.2 0.3 select_reduce_fusion.1
  2.4 0.1 copy.21
  2.5 0.1 reshape.180
  2.7 0.0 copy-done
  2.7 0.1 dynamic-slice_bitcast_fusion.2
  2.7 0.7 pad_add_fusion
  3.4 0.1 copy.22
  3.5 0.6 gather_fusion
  4.1 0.1 reshape.181
  4.2 0.7 pad_add_fusion.1.table_ref
  4.9 1.0 pad_maximum_fusion
  5.9 0.0 copy-start.1
  5.9 0.8 gather_fusion.1
  6.7 0.8 copy.24
  7.6 0.0 copy-done.1
  7.6 0.6 scatter.4.class_ref
  8.2 106.8 %filter_round.1 = (bf16[24,4096]{1,0:T(8,128)(2,1)}, f32[1,512]{1,0:T(1,128)}) custom-call(s32[288]{0:T(512)} %pad_add_fusion.1.table_ref, f32[2]{0:T(128)} %class_bias_ref.1, bf16[4,12,40,128]{3,2,1,0:T(8,128)(2,1)} %bitcast.22, bf16[1,96,16,512]{3,2,1,0:T(8,128)(2,1)} %keys_hbm.1, bf16[1,96,16,512]{3,2,1,0:T(8,128)(2,1)} %values_hbm.1, ...), custom_call_target="tpu_custom_call" | custom-call | tf_op jit(solution)/shard_map/filter_round/pallas_call | solution.py:526
  115.0 1.6 %copy.27 = bf16[1,24,4096]{2,1,0:T(8,128)(2,1)} copy(bf16[1,24,4096]{2,1,0:T(8,128)(2,1)} %bitcast.23) | data formatting | bytes 393216
  116.7 1.2 %copy.28 = f32[512]{0:T(512)} copy(f32[512]{0:T(512)} %bitcast.30) | data formatting | bytes 4096
  (9 shorter events, 0.1 us)
Async XLA Ops:
  0.6 2.0 %copy-start = (s32[96]{0:T(128)S(1)}, s32[96]{0:T(128)}, u32[]{:S(2)}) copy-start(s32[96]{0:T(128)} %param.23) | copy-start | bytes 1156
  5.9 1.7 %copy-start.1 = (bf16[2048,2]{0,1:T(2,128)(2,1)S(1)}, bf16[2048,2]{0,1:T(2,128)(2,1)}, u32[]{:S(2)}) copy-start(bf16[2048,2]{0,1:T(2,128)(2,1)} %param.28) | copy-start | bytes 24580

commit v3 on v1

--- a/solution.py
+++ b/solution.py
@@ -267,8 +267,6 @@
         return carry
 
     lax.fori_loop(0, nb * blocks, serve_block, 0)
-    for d in range(1, nb):
-        back(d).start()
     own_back = pltpu.make_async_copy(served_out.at[z], returned.at[z], local_sem.at[4])
     own_back.start()
 
@@ -367,6 +365,9 @@
 
         lax.fori_loop(1, nb - 1, near, 0)
         line_step(nb - 1, n)
+        if n == 0:
+            for d in range(1, nb):
+                back(d).start()
 
     for n in range(chunks):
         multiply_at(nb - 1, n)

time: 118 us -> 118 us (level)
  no operation moved by 1% of the time
where the time goes in v3:
time: 118 us; the launch traced here: 117 us
  Pallas kernels  106 us (90%)
  local copies, waits for them, and re-layouts  5.89 us (5%)
  other arithmetic  4.74 us (4%)
    pallas_call x1, Pallas kernels, per_device(): pl.pallas_call(functools.partial(fused_kernel, dims), out_shape=(jax.Shap...  106 us

profile of v3, /device:TPU:0, one launch (start us, length us, event | category | flops | bytes accessed | tf_op | source)
XLA Modules:
  0.0 117.1 jit_solution(5928056943215929960)
XLA Ops:
  0.6 0.0 copy-start
  0.6 0.7 and_select_fusion
  1.3 0.1 reshape.173
  1.4 0.2 convert_reduce_fusion
  1.6 0.0 copy-done
  1.7 0.1 dynamic-slice_bitcast_fusion.2
  1.7 0.7 pad_add_fusion
  2.4 0.1 copy.22
  2.5 0.3 select_reduce_fusion.1
  2.8 0.1 copy.21
  2.9 0.1 reshape.182
  3.0 0.6 gather_fusion
  3.6 0.1 reshape.174
  3.7 0.7 pad_add_fusion.1.table_ref
  4.4 1.0 pad_maximum_fusion
  5.4 0.3 select_reduce_fusion
  5.7 0.1 copy.24
  5.8 0.1 reshape.175
  5.9 0.0 copy-start.1
  5.9 0.8 gather_fusion.1
  6.7 0.1 copy.25
  6.8 0.1 copy.23
  6.9 0.9 broadcast_select_fusion.mail_ref
  7.8 0.0 copy-done.1
  7.8 0.6 scatter.4.class_ref
  8.4 105.8 %filter_round.1 = (bf16[24,32,128]{2,1,0:T(8,128)(2,1)}, f32[1,512]{1,0:T(1,128)}) custom-call(s32[288]{0:T(512)} %pad_add_fusion.1.table_ref, f32[2]{0:T(128)} %class_bias_ref.1, bf16[4,12,40,128]{3,2,1,0:T(8,128)(2,1)} %broadcast_select_fusion.mail_ref, bf16[1,96,16,512]{3,2,1,0:T(8,128)(2,1)} %keys_hbm.1, bf16[1,96,16,512]{3,2,1,0:T(8,128)(2,1)} %values_hbm.1, ...), custom_call_target="tpu_custom_call" | custom-call | tf_op jit(solution)/shard_map/filter_round/pallas_call | solution.py:509
  114.2 1.7 %reshape.178 = bf16[1,24,4096]{2,1,0:T(8,128)(2,1)} reshape(bf16[24,32,128]{2,1,0:T(8,128)(2,1)} %get-tuple-element.16) | data formatting | bytes 393216 | tf_op jit(solution)/shard_map/reshape | solution.py:563
  115.9 1.2 %copy.27 = f32[512]{0:T(512)} copy(f32[512]{0:T(512)} %bitcast.30) | data formatting | bytes 4096
  (10 shorter events, 0.1 us)
Async XLA Ops:
  0.6 1.0 copy-start
  5.9 1.9 %copy-start.1 = (bf16[2048,2]{0,1:T(2,128)(2,1)S(1)}, bf16[2048,2]{0,1:T(2,128)(2,1)}, u32[]{:S(2)}) copy-start(bf16[2048,2]{0,1:T(2,128)(2,1)} %param.28) | copy-start | bytes 24580
